TPU v7x, 128 devices: a whole 4x4x4 slice. The times are simulated.
128 devices in a mesh: gz: 8 (over z, y_lo), gy: 16 (over x, y_hi, core).
Axes of the slice: x: 4, y: 4 (y_hi: 2, y_lo: 2; y = y_hi * 2 + y_lo), z: 4, core: 2. Of those that a mesh axis runs over, the one named last changes fastest.
Arguments:
- thermal_departure: float32 [8, 2048, 2048], P(None, 'gy', 'gz'), may hold values from -6 to 6
- speed_along_primary: float32 [8, 2048, 2048], P(None, 'gy', 'gz'), may hold values from -4 to 4
- speed_along_lateral: float32 [8, 2048, 2048], P(None, 'gy', 'gz'), may hold values from -4 to 4
- upward_speed: float32 [8, 2048, 2048], P(None, 'gy', 'gz'), may hold values from -4 to 4
- container_solid_markers: int32 [8, 2048, 2048], P(None, 'gy', 'gz'), may hold values 0 or 1
Outputs:
- temp_next: float32 [8, 2048, 2048], P(None, 'gy', 'gz')
- u_next: float32 [8, 2048, 2048], P(None, 'gy', 'gz')
- v_next: float32 [8, 2048, 2048], P(None, 'gy', 'gz')
- w_next: float32 [8, 2048, 2048], P(None, 'gy', 'gz')
- path_map: float32 [8, 2048], P('gz', 'gy')
Inputs may be any that keep to these rules, and one draw needn't show every extreme that they name: `container_solid_markers`: 1 marks air, 0 a solid cell.
All inputs are finite; a program needn't handle non-finite values. No bound on the sum of `container_solid_markers` on one device may be relied on, other than what follows from the above.
Results may differ from a plain program's by a relative error of at most 0.00002.
Values sent between devices are 32-bit elements; how exact they have to be, the bound alone decides.
A program may use at most 128 MiB of HBM per device.

v0:
```python
import math

import jax
import jax.numpy as jnp
from jax import lax
from jax.sharding import PartitionSpec as P

TIME_STEP = 0.1
NU_BASE = 0.05
KAPPA_BASE = 0.05
SMAG_COEF = 0.03
PRANDTL = 0.4
BUOYANCY = 0.5


def extended(shard, sides, width, wrap):
    for axis, dim in sides:
        count, length = (lax.axis_size(axis), shard.shape[dim])
        up = [(i, (i + 1) % count) for i in range(count if wrap else count - 1)]
        down = [(j, i) for i, j in up]
        last = lax.slice_in_dim(shard, length - width, length, axis=dim)
        first = lax.slice_in_dim(shard, 0, width, axis=dim)
        before = lax.ppermute(last, axis, up)
        after = lax.ppermute(first, axis, down)
        shard = jnp.concatenate([before, shard, after], axis=dim)
    return shard


def tendencies(padded):
    centre = padded[:, :, 1:-1, 1:-1]
    east_side = jnp.roll(centre, -1, 1)
    west_side = jnp.roll(centre, 1, 1)
    north_side = padded[:, :, 2:, 1:-1]
    south_side = padded[:, :, :-2, 1:-1]
    upper_side = padded[:, :, 1:-1, 2:]
    lower_side = padded[:, :, 1:-1, :-2]
    grad_x = 0.5 * (east_side - west_side)
    grad_y = 0.5 * (north_side - south_side)
    grad_z = 0.5 * (upper_side - lower_side)
    laplace = (
        east_side + west_side + north_side + south_side + upper_side + lower_side - 6.0 * centre
    )
    advect = centre[1] * grad_x + centre[2] * grad_y + centre[3] * grad_z
    strain = grad_x[1] * grad_x[1] + grad_y[2] * grad_y[2] + grad_z[3] * grad_z[3]
    shear_a = grad_y[1] + grad_x[2]
    shear_b = grad_z[1] + grad_x[3]
    shear_c = grad_z[2] + grad_y[3]
    strain = strain + 0.5 * (shear_a * shear_a + shear_b * shear_b + shear_c * shear_c)
    eddy_visc = SMAG_COEF * jnp.sqrt(2.0 * strain + 0.01)
    diffusion = jnp.stack(
        [
            KAPPA_BASE + eddy_visc / PRANDTL,
            NU_BASE + eddy_visc,
            NU_BASE + eddy_visc,
            NU_BASE + eddy_visc,
        ]
    )
    tendency = diffusion * laplace - advect
    buoyant = tendency[3] + BUOYANCY * centre[0]
    return jnp.stack([tendency[0], tendency[1], tendency[2], buoyant])


def masked(fluid_unknowns, fluid_mask):
    return jnp.concatenate([fluid_unknowns[:1], fluid_unknowns[1:] * fluid_mask[None]], 0)


def pad_one(fluid_unknowns):
    widened = extended(fluid_unknowns, (("gy", 2),), 1, True)
    return extended(widened, (("gz", 3),), 1, False)


def on_device(
    thermal_departure,
    speed_along_primary,
    speed_along_lateral,
    upward_speed,
    container_solid_markers,
):
    fluid_mask = container_solid_markers.astype(jnp.float32)
    fluid_unknowns = jnp.stack(
        [thermal_departure, speed_along_primary, speed_along_lateral, upward_speed]
    )
    column_cells = fluid_unknowns.shape[3]
    height_count = lax.axis_size("gz")
    section_one = masked(
        fluid_unknowns + TIME_STEP * tendencies(pad_one(fluid_unknowns)), fluid_mask
    )
    section_two = masked(
        0.5 * fluid_unknowns + 0.5 * (section_one + TIME_STEP * tendencies(pad_one(section_one))),
        fluid_mask,
    )
    refraction = 8.0 * (1.0 - jnp.exp(-section_two[0] / 8.0))
    scale_factor = 1.0 / math.sqrt(column_cells * height_count)
    path_sum = lax.psum_scatter(jnp.sum(refraction, axis=2), "gz", scatter_dimension=0, tiled=True)
    path_map = path_sum * scale_factor
    return (section_two[0], section_two[1], section_two[2], section_two[3], path_map)


def solution(mesh):
    return jax.shard_map(
        on_device,
        mesh=mesh,
        in_specs=(
            P(None, "gy", "gz"),
            P(None, "gy", "gz"),
            P(None, "gy", "gz"),
            P(None, "gy", "gz"),
            P(None, "gy", "gz"),
        ),
        out_specs=(
            P(None, "gy", "gz"),
            P(None, "gy", "gz"),
            P(None, "gy", "gz"),
            P(None, "gy", "gz"),
            P("gz", "gy"),
        ),
        check_vma=False,
    )
```

profile of v0, /device:TPU:0, one launch (start us, length us, event | category | flops | bytes accessed | tf_op | source)
XLA Modules:
  0.0 178.8 jit_solution(12460911946854210109)
XLA Ops:
  0.7 3.0 %copy_multiply_fusion.2 = (f32[8,128,256]{2,0,1:T(8,128)}, f32[1,8,128,256]{3,1,2,0:T(8,128)S(1)}) fusion(f32[8,128,256]{2,1,0:T(8,128)} %param.6), kind=kLoop, calls=%fused_computation.135 | loop fusion | flops 262144 | bytes 3145728 | tf_op jit(solution)/shard_map/mul | solution.py:43
  3.7 2.2 %copy.74 = f32[8,128,256]{2,0,1:T(8,128)S(1)} copy(f32[8,128,256]{2,1,0:T(8,128)} %param.5) | data formatting | bytes 2097152 | tf_op args[0]
  5.9 2.7 %copy_multiply_fusion = (f32[8,128,256]{2,0,1:T(8,128)}, f32[1,8,128,256]{3,1,2,0:T(8,128)S(1)}, f32[1,8,128,256]{3,1,2,0:T(8,128)S(1)}, f32[8,128,256]{2,0,1:T(8,128)}) fusion(f32[8,128,256]{2,1,0:T(8,128)S(1)} %copy-done.35, f32[8,128,256]{2,1,0:T(8,128)S(1)} %copy-done.36), kind=kLoop, calls=%fused_computation.131 | loop fusion | flops 524288 | bytes 6291456 | tf_op jit(solution)/shard_map/mul | solution.py:43
  9.6 4.9 %collective-permute-start = (f32[4,8,1,256]{3,1,2,0:T(8,128)S(1)}, f32[4,8,1,256]{3,1,2,0:T(8,128)S(1)}, u32[]{:S(2)}, u32[]{:S(2)}) collective-permute-start(f32[4,8,1,256]{3,1,2,0:T(8,128)S(1)} %get-tuple-element.41), channel_id=1, source_target_pairs={{1,0},{2,1},{3,2},{4,3},{5,4},{6,5},{7,6},{8,7},{9,8},{10,9},{11,1... | collective-permute-start | bytes 98312 | tf_op jit(solution)/shard_map/ppermute | solution.py:24
  16.0 4.2 %fusion.11 = f32[4,8,128,256]{3,1,2,0:T(8,128)} fusion(f32[4,7,128,256]{3,1,2,0:T(8,128)S(1)} %get-tuple-element.37, f32[4,1,128,256]{3,1,2,0:T(1,128)S(1)} %get-tuple-element.39, f32[4,1,128,256]{3,1,2,0:T(1,128)S(1)} %get-tuple-element.38, f32[4,7,128,256]{3,1,2,0:T(8,128)S(1)} %get-tuple-element.36), kind=kLoop, calls=%fused_computation.67 | loop fusion | flops 4194304 | bytes 12582912 | tf_op jit(solution)/shard_map/mul | solution.py:37
  20.3 1.6 copy.56
  24.1 2.6 %fusion.51 = (f32[4,8,130,1]{3,1,2,0:T(8,128)}, f32[4,8,130,1]{3,1,2,0:T(8,128)}) fusion(f32[4,8,130,256]{3,1,2,0:T(8,128)S(1)} %pad_maximum_fusion.1), kind=kLoop, calls=%fused_computation.144 | loop fusion | bytes 66560 | tf_op jit(solution)/shard_map/slice | solution.py:21
  26.7 2.8 %copy.48 = f32[4,8,130,1]{2,1,3,0:T(8,128)S(1)} copy(f32[4,8,130,1]{3,1,2,0:T(8,128)} %get-tuple-element.29) | data formatting | bytes 33280 | tf_op jit(solution)/shard_map/slice | solution.py:22
  30.9 2.8 %copy.50 = f32[4,8,130,1]{2,1,3,0:T(8,128)S(1)} copy(f32[4,8,130,1]{3,1,2,0:T(8,128)} %get-tuple-element.28) | data formatting | bytes 33280 | tf_op jit(solution)/shard_map/slice | solution.py:21
  33.7 4.7 %collective-permute-start.3 = (f32[4,8,130,1]{2,1,3,0:T(8,128)S(1)}, f32[4,8,130,1]{2,1,3,0:T(8,128)S(1)}, u32[]{:S(2)}, u32[]{:S(2)}) collective-permute-start(f32[4,8,130,1]{2,1,3,0:T(8,128)S(1)} %copy.50), channel_id=1, source_target_pairs={{0,16},{16,32},{32,48},{48,64},{64,80},{80,96},{96,112},{1,17},{17... | collective-permute-start | bytes 49928 | tf_op jit(solution)/shard_map/ppermute | solution.py:23
  38.5 3.5 %broadcast_multiply_fusion.2 = f32[4,8,128,256]{3,1,2,0:T(8,128)} fusion(f32[4,8,1,256]{3,1,2,0:T(8,128)S(1)} %collective-permute-done, f32[1,8,128,256]{3,1,2,0:T(8,128)S(1)} %get-tuple-element.53, f32[1,8,128,256]{3,1,2,0:T(8,128)} %copy-done.8, f32[1,8,128,256]{3,1,2,0:T(8,128)S(1)} %get-tuple-element.49, f32[1,8,128,256]{3,1,2,0:T(8,128)S(1)} %bitcast.36, ...), kind=kLoop, calls=%fused_computation.74 | loop fusion | flops 10485760 | bytes 8454144 | tf_op jit(solution)/shard_map/mul | solution.py:38
  41.9 2.6 %copy.49 = f32[4,8,130,1]{3,1,2,0:T(8,128)} copy(f32[4,8,130,1]{2,1,3,0:T(8,128)S(1)} %collective-permute-done.2) | data formatting | bytes 33280 | tf_op jit(solution)/shard_map/ppermute | solution.py:24
  44.5 2.6 %copy.51 = f32[4,8,130,1]{3,1,2,0:T(8,128)} copy(f32[4,8,130,1]{2,1,3,0:T(8,128)S(1)} %collective-permute-done.3) | data formatting | bytes 33280 | tf_op jit(solution)/shard_map/ppermute | solution.py:23
  47.1 9.7 %broadcast_multiply_fusion.1 = f32[4,8,128,256]{3,1,2,0:T(8,128)S(1)} fusion(f32[4,8,130,1]{3,1,2,0:T(8,128)} %copy.49, f32[4,8,1,256]{3,1,2,0:T(8,128)S(1)} %collective-permute-done, f32[1,8,128,256]{3,1,2,0:T(8,128)S(1)} %get-tuple-element.53, f32[1,8,128,256]{3,1,2,0:T(8,128)} %copy-done.8, f32[1,8,128,256]{3,1,2,0:T(8,128)S(1)} %get-tuple-element.49, ...), kind=kLoop, calls=%fused_computation.73 | loop fusion | flops 14680064 | bytes 8487424 | tf_op jit(solution)/shard_map/mul | solution.py:39
  56.9 1.9 %multiply_add_fusion.3 = (f32[1,8,128,256]{3,1,2,0:T(8,128)}, f32[1,8,128,256]{3,1,2,0:T(8,128)S(1)}) fusion(f32[4,8,128,256]{3,1,2,0:T(8,128)S(1)} %copy-done.24, f32[4,8,128,256]{3,1,2,0:T(8,128)S(1)} %broadcast_multiply_fusion.1, f32[4,8,128,256]{3,1,2,0:T(8,128)S(1)} %copy-done.22), kind=kLoop, calls=%fused_computation.130 | loop fusion | flops 4980736 | bytes 11534336 | tf_op jit(solution)/shard_map/add | solution.py:52
  61.8 11.1 %fusion.2 = f32[4,8,128,256]{3,1,2,0:T(8,128)S(1)} fusion(f32[1,8,128,256]{3,1,2,0:T(8,128)S(1)} %multiply_add_fusion.2, f32[1,8,128,256]{3,1,2,0:T(8,128)} %get-tuple-element.22, f32[4,7,128,256]{3,1,2,0:T(8,128)S(1)} %copy-done.16, f32[4,1,128,256]{3,1,2,0:T(1,128)S(1)} %copy-done.32, f32[4,1,128,256]{3,1,2,0:T(1,128)S(1)} %copy-done.30, ...), kind=kLoop, calls=%fused_computation.53 | loop fusion | flops 47185920 | bytes 22118912 | tf_op jit(solution)/shard_map/sub | solution.py:58
  75.6 1.9 %copy-done.17 = f32[4,8,128,256]{3,1,2,0:T(8,128)} copy-done((f32[4,8,128,256]{3,1,2,0:T(8,128)}, f32[4,8,128,256]{3,1,2,0:T(8,128)S(1)}, u32[]{:S(2)}) %copy-start.17) | copy-done | bytes 4194328
  77.8 3.8 %fusion = (f32[4,7,128,256]{3,1,2,0:T(8,128)}, f32[4,7,128,256]{3,1,2,0:T(8,128)}) fusion(f32[3,8,128,256]{3,1,2,0:T(8,128)S(1)} %slice_multiply_fusion.1, f32[1,8,128,256]{3,1,2,0:T(8,128)S(1)} %slice.267), kind=kLoop, calls=%fused_computation.15 | loop fusion | flops 1835008 | bytes 11534336 | tf_op jit(solution)/shard_map/concatenate | solution.py:64
  81.6 1.7 fusion.17
  83.3 4.8 %collective-permute-start.4 = (f32[4,8,1,256]{3,1,2,0:T(8,128)S(1)}, f32[4,8,1,256]{3,1,2,0:T(8,128)S(1)}, u32[]{:S(2)}, u32[]{:S(2)}) collective-permute-start(f32[4,8,1,256]{3,1,2,0:T(8,128)S(1)} %get-tuple-element.35), channel_id=1, source_target_pairs={{1,0},{2,1},{3,2},{4,3},{5,4},{6,5},{7,6},{8,7},{9,8},{10,9},{11,1... | collective-permute-start | bytes 98312 | tf_op jit(solution)/shard_map/ppermute | solution.py:24
  89.7 5.4 %collective-permute-done.5 = f32[4,8,1,256]{3,1,2,0:T(8,128)S(1)} collective-permute-done((f32[4,8,1,256]{3,1,2,0:T(8,128)S(1)}, f32[4,8,1,256]{3,1,2,0:T(8,128)S(1)}, u32[]{:S(2)}, u32[]{:S(2)}) %collective-permute-start.5) | collective-permute-done | bytes 32800 | tf_op jit(solution)/shard_map/ppermute | solution.py:23
  95.4 2.6 %fusion.50 = (f32[4,8,130,1]{3,1,2,0:T(8,128)}, f32[4,8,130,1]{3,1,2,0:T(8,128)}) fusion(f32[4,8,130,256]{3,1,2,0:T(8,128)S(1)} %pad_maximum_fusion.2), kind=kLoop, calls=%fused_computation.143 | loop fusion | bytes 66560 | tf_op jit(solution)/shard_map/slice | solution.py:21
  98.0 2.8 %copy.57 = f32[4,8,130,1]{2,1,3,0:T(8,128)S(1)} copy(f32[4,8,130,1]{3,1,2,0:T(8,128)} %get-tuple-element.27) | data formatting | bytes 33280 | tf_op jit(solution)/shard_map/slice | solution.py:22
  102.3 2.8 %copy.59 = f32[4,8,130,1]{2,1,3,0:T(8,128)S(1)} copy(f32[4,8,130,1]{3,1,2,0:T(8,128)} %get-tuple-element.26) | data formatting | bytes 33280 | tf_op jit(solution)/shard_map/slice | solution.py:21
  105.2 4.5 %collective-permute-start.7 = (f32[4,8,130,1]{2,1,3,0:T(8,128)S(1)}, f32[4,8,130,1]{2,1,3,0:T(8,128)S(1)}, u32[]{:S(2)}, u32[]{:S(2)}) collective-permute-start(f32[4,8,130,1]{2,1,3,0:T(8,128)S(1)} %copy.59), channel_id=1, source_target_pairs={{0,16},{16,32},{32,48},{48,64},{64,80},{80,96},{96,112},{1,17},{17... | collective-permute-start | bytes 49928 | tf_op jit(solution)/shard_map/ppermute | solution.py:23
  109.7 7.5 %fusion.9 = f32[4,8,128,256]{3,1,2,0:T(8,128)} fusion(f32[4,7,128,256]{3,1,2,0:T(8,128)} %get-tuple-element.31, f32[4,1,128,256]{3,1,2,0:T(1,128)} %get-tuple-element.33, f32[4,1,128,256]{3,1,2,0:T(1,128)} %get-tuple-element.32, f32[4,7,128,256]{3,1,2,0:T(8,128)} %get-tuple-element.30), kind=kLoop, calls=%fused_computation.65 | loop fusion | flops 4194304 | bytes 12582912 | tf_op jit(solution)/shard_map/mul | solution.py:37
  117.2 2.6 %copy.58 = f32[4,8,130,1]{3,1,2,0:T(8,128)} copy(f32[4,8,130,1]{2,1,3,0:T(8,128)S(1)} %collective-permute-done.6) | data formatting | bytes 33280 | tf_op jit(solution)/shard_map/ppermute | solution.py:24
  119.8 2.6 %copy.60 = f32[4,8,130,1]{3,1,2,0:T(8,128)} copy(f32[4,8,130,1]{2,1,3,0:T(8,128)S(1)} %collective-permute-done.7) | data formatting | bytes 33280 | tf_op jit(solution)/shard_map/ppermute | solution.py:23
  122.4 10.3 %broadcast_multiply_fusion = (f32[4,8,128,256]{3,1,2,0:T(8,128)S(1)}, f32[4,8,128,256]{3,1,2,0:T(8,128)}) fusion(f32[4,8,130,1]{3,1,2,0:T(8,128)} %copy.58, f32[4,8,1,256]{3,1,2,0:T(8,128)S(1)} %collective-permute-done.4, f32[3,8,128,256]{3,1,2,0:T(8,128)S(1)} %slice_multiply_fusion.1, f32[1,8,128,256]{3,1,2,0:T(8,128)} %copy-done, ...), kind=kLoop, calls=%fused_computation.72 | loop fusion | flops 16777216 | bytes 12681728 | tf_op jit(solution)/shard_map/mul | solution.py:39
  132.8 3.9 %multiply_add_fusion.1 = (f32[1,8,128,256]{3,1,2,0:T(8,128)}, f32[1,8,128,256]{3,1,2,0:T(8,128)S(1)}) fusion(f32[4,8,128,256]{3,1,2,0:T(8,128)} %get-tuple-element.25, f32[4,8,128,256]{3,1,2,0:T(8,128)S(1)} %get-tuple-element.24, f32[4,8,128,256]{3,1,2,0:T(8,128)S(1)} %copy-done.23), kind=kLoop, calls=%fused_computation.128 | loop fusion | flops 4980736 | bytes 11534336 | tf_op jit(solution)/shard_map/add | solution.py:52
  138.6 9.6 %fusion.4 = f32[4,8,128,256]{3,1,2,0:T(8,128)S(1)} fusion(f32[1,8,128,256]{3,1,2,0:T(8,128)S(1)} %multiply_add_fusion, f32[1,8,128,256]{3,1,2,0:T(8,128)} %get-tuple-element.20, f32[3,8,128,256]{3,1,2,0:T(8,128)S(1)} %slice_multiply_fusion.1, f32[1,8,128,256]{3,1,2,0:T(8,128)S(1)} %copy-done.1, f32[4,7,128,256]{3,1,2,0:T(8,128)S(1)} %copy-done.12, ...), kind=kLoop, calls=%fused_computation.59 | loop fusion | flops 36700160 | bytes 22118912 | tf_op jit(solution)/shard_map/sub | solution.py:58
  158.0 19.7 %all-reduce = f32[8,128]{1,0:T(8,128)S(1)} all-reduce(f32[8,128]{1,0:T(8,128)S(1)} %copy.61), channel_id=2, replica_groups=mesh['gz'=8,'gy'=16] {'gz'}, use_global_device_ids=true, to_apply=%region_1.2.clone | all-reduce | flops 1024 | bytes 8192
  (116 shorter events, 28.1 us)
Async XLA Ops:
  0.6 5.3 %copy-start.36 = (f32[8,128,256]{2,1,0:T(8,128)S(1)}, f32[8,128,256]{2,1,0:T(8,128)}, u32[]{:S(2)}) copy-start(f32[8,128,256]{2,1,0:T(8,128)} %param.7) | copy-start | bytes 3145732
  0.6 5.3 %copy-start.35 = (f32[8,128,256]{2,1,0:T(8,128)S(1)}, f32[8,128,256]{2,1,0:T(8,128)}, u32[]{:S(2)}) copy-start(f32[8,128,256]{2,1,0:T(8,128)} %param.8) | copy-start | bytes 3145732
  3.7 71.2 %copy-start.2 = (f32[1,8,128,256]{3,1,2,0:T(8,128)}, f32[1,8,128,256]{3,1,2,0:T(8,128)S(1)}, u32[]{:S(2)}) copy-start(f32[1,8,128,256]{3,1,2,0:T(8,128)S(1)} %get-tuple-element.49) | copy-start | bytes 3145732
  5.9 68.9 %copy-start.4 = (f32[8,128,256]{2,0,1:T(8,128)}, f32[8,128,256]{2,0,1:T(8,128)S(1)}, u32[]{:S(2)}) copy-start(f32[8,128,256]{2,0,1:T(8,128)S(1)} %copy.74) | copy-start | bytes 3145732
  8.6 66.3 %copy-start.6 = (f32[1,8,128,256]{3,1,2,0:T(8,128)}, f32[1,8,128,256]{3,1,2,0:T(8,128)S(1)}, u32[]{:S(2)}) copy-start(f32[1,8,128,256]{3,1,2,0:T(8,128)S(1)} %get-tuple-element.53) | copy-start | bytes 3145732
  9.6 13.1 %collective-permute-start = (f32[4,8,1,256]{3,1,2,0:T(8,128)S(1)}, f32[4,8,1,256]{3,1,2,0:T(8,128)S(1)}, u32[]{:S(2)}, u32[]{:S(2)}) collective-permute-start(f32[4,8,1,256]{3,1,2,0:T(8,128)S(1)} %get-tuple-element.41), channel_id=1, source_target_pairs={{1,0},{2,1},{3,2},{4,3},{5,4},{6,5},{7,6},{8,7},{9,8},{10,9},{11,1... | collective-permute-start | bytes 98312 | tf_op jit(solution)/shard_map/ppermute | solution.py:24
  14.5 8.1 %collective-permute-start.1 = (f32[4,8,1,256]{3,1,2,0:T(8,128)S(1)}, f32[4,8,1,256]{3,1,2,0:T(8,128)S(1)}, u32[]{:S(2)}, u32[]{:S(2)}) collective-permute-start(f32[4,8,1,256]{3,1,2,0:T(8,128)S(1)} %get-tuple-element.40), channel_id=1, source_target_pairs={{0,1},{1,2},{2,3},{3,4},{4,5},{5,6},{6,7},{7,8},{8,9},{9,10},{10,1... | collective-permute-start | bytes 98312 | tf_op jit(solution)/shard_map/ppermute | solution.py:23
  15.3 4.9 %copy-start.13 = (f32[4,7,128,256]{3,1,2,0:T(8,128)}, f32[4,7,128,256]{3,1,2,0:T(8,128)S(1)}, u32[]{:S(2)}) copy-start(f32[4,7,128,256]{3,1,2,0:T(8,128)S(1)} %get-tuple-element.36) | copy-start | bytes 11010052
  15.3 4.9 %copy-start.15 = (f32[4,7,128,256]{3,1,2,0:T(8,128)}, f32[4,7,128,256]{3,1,2,0:T(8,128)S(1)}, u32[]{:S(2)}) copy-start(f32[4,7,128,256]{3,1,2,0:T(8,128)S(1)} %get-tuple-element.37) | copy-start | bytes 11010052
  15.9 4.2 %copy-start.29 = (f32[4,1,128,256]{3,1,2,0:T(1,128)}, f32[4,1,128,256]{3,1,2,0:T(1,128)S(1)}, u32[]{:S(2)}) copy-start(f32[4,1,128,256]{3,1,2,0:T(1,128)S(1)} %get-tuple-element.38) | copy-start | bytes 1572868
  16.0 4.2 %copy-start.31 = (f32[4,1,128,256]{3,1,2,0:T(1,128)}, f32[4,1,128,256]{3,1,2,0:T(1,128)S(1)}, u32[]{:S(2)}) copy-start(f32[4,1,128,256]{3,1,2,0:T(1,128)S(1)} %get-tuple-element.39) | copy-start | bytes 1572868
  16.0 4.2 %copy-start.34 = (s32[8,128,256]{2,1,0:T(8,128)S(1)}, s32[8,128,256]{2,1,0:T(8,128)}, u32[]{:S(2)}) copy-start(s32[8,128,256]{2,1,0:T(8,128)} %param.9) | copy-start | bytes 3145732
  29.6 12.4 %collective-permute-start.2 = (f32[4,8,130,1]{2,1,3,0:T(8,128)S(1)}, f32[4,8,130,1]{2,1,3,0:T(8,128)S(1)}, u32[]{:S(2)}, u32[]{:S(2)}) collective-permute-start(f32[4,8,130,1]{2,1,3,0:T(8,128)S(1)} %copy.48), channel_id=1, source_target_pairs={{16,0},{32,16},{48,32},{64,48},{80,64},{96,80},{112,96},{17,1},{33... | collective-permute-start | bytes 49928 | tf_op jit(solution)/shard_map/ppermute | solution.py:24
  33.7 10.8 %collective-permute-start.3 = (f32[4,8,130,1]{2,1,3,0:T(8,128)S(1)}, f32[4,8,130,1]{2,1,3,0:T(8,128)S(1)}, u32[]{:S(2)}, u32[]{:S(2)}) collective-permute-start(f32[4,8,130,1]{2,1,3,0:T(8,128)S(1)} %copy.50), channel_id=1, source_target_pairs={{0,16},{16,32},{32,48},{48,64},{64,80},{80,96},{96,112},{1,17},{17... | collective-permute-start | bytes 49928 | tf_op jit(solution)/shard_map/ppermute | solution.py:23
  47.1 9.7 %copy-start.22 = (f32[4,8,128,256]{3,1,2,0:T(8,128)S(1)}, f32[4,8,128,256]{3,1,2,0:T(8,128)}, u32[]{:S(2)}) copy-start(f32[4,8,128,256]{3,1,2,0:T(8,128)} %fusion.11) | copy-start | bytes 12582916
  47.1 9.7 %copy-start.24 = (f32[4,8,128,256]{3,1,2,0:T(8,128)S(1)}, f32[4,8,128,256]{3,1,2,0:T(8,128)}, u32[]{:S(2)}) copy-start(f32[4,8,128,256]{3,1,2,0:T(8,128)} %broadcast_multiply_fusion.2) | copy-start | bytes 12582916
  47.1 11.8 %copy-start.19 = (f32[4,8,130,1]{3,1,2,0:T(8,128)S(1)}, f32[4,8,130,1]{3,1,2,0:T(8,128)}, u32[]{:S(2)}) copy-start(f32[4,8,130,1]{3,1,2,0:T(8,128)} %copy.51) | copy-start | bytes 49924
  56.9 4.1 %copy-start.16 = (f32[4,7,128,256]{3,1,2,0:T(8,128)S(1)}, f32[4,7,128,256]{3,1,2,0:T(8,128)}, u32[]{:S(2)}) copy-start(f32[4,7,128,256]{3,1,2,0:T(8,128)} %copy-done.15) | copy-start | bytes 11010052
  56.9 4.7 %copy-start.18 = (f32[4,8,130,1]{3,1,2,0:T(8,128)S(1)}, f32[4,8,130,1]{3,1,2,0:T(8,128)}, u32[]{:S(2)}) copy-start(f32[4,8,130,1]{3,1,2,0:T(8,128)} %copy.49) | copy-start | bytes 49924
  56.9 4.7 %copy-start.30 = (f32[4,1,128,256]{3,1,2,0:T(1,128)S(1)}, f32[4,1,128,256]{3,1,2,0:T(1,128)}, u32[]{:S(2)}) copy-start(f32[4,1,128,256]{3,1,2,0:T(1,128)} %copy-done.29) | copy-start | bytes 1572868
  56.9 4.9 %copy-start.32 = (f32[4,1,128,256]{3,1,2,0:T(1,128)S(1)}, f32[4,1,128,256]{3,1,2,0:T(1,128)}, u32[]{:S(2)}) copy-start(f32[4,1,128,256]{3,1,2,0:T(1,128)} %copy-done.31) | copy-start | bytes 1572868
  77.5 17.6 %copy-start = (f32[1,8,128,256]{3,1,2,0:T(8,128)}, f32[1,8,128,256]{3,1,2,0:T(8,128)S(1)}, u32[]{:S(2)}) copy-start(f32[1,8,128,256]{3,1,2,0:T(8,128)S(1)} %slice.267) | copy-start | bytes 3145732
  83.3 6.4 %collective-permute-start.4 = (f32[4,8,1,256]{3,1,2,0:T(8,128)S(1)}, f32[4,8,1,256]{3,1,2,0:T(8,128)S(1)}, u32[]{:S(2)}, u32[]{:S(2)}) collective-permute-start(f32[4,8,1,256]{3,1,2,0:T(8,128)S(1)} %get-tuple-element.35), channel_id=1, source_target_pairs={{1,0},{2,1},{3,2},{4,3},{5,4},{6,5},{7,6},{8,7},{9,8},{10,9},{11,1... | collective-permute-start | bytes 98312 | tf_op jit(solution)/shard_map/ppermute | solution.py:24
  88.1 7.0 %collective-permute-start.5 = (f32[4,8,1,256]{3,1,2,0:T(8,128)S(1)}, f32[4,8,1,256]{3,1,2,0:T(8,128)S(1)}, u32[]{:S(2)}, u32[]{:S(2)}) collective-permute-start(f32[4,8,1,256]{3,1,2,0:T(8,128)S(1)} %get-tuple-element.34), channel_id=1, source_target_pairs={{0,1},{1,2},{2,3},{3,4},{4,5},{5,6},{6,7},{7,8},{8,9},{9,10},{10,1... | collective-permute-start | bytes 98312 | tf_op jit(solution)/shard_map/ppermute | solution.py:23
  100.8 16.4 %collective-permute-start.6 = (f32[4,8,130,1]{2,1,3,0:T(8,128)S(1)}, f32[4,8,130,1]{2,1,3,0:T(8,128)S(1)}, u32[]{:S(2)}, u32[]{:S(2)}) collective-permute-start(f32[4,8,130,1]{2,1,3,0:T(8,128)S(1)} %copy.57), channel_id=1, source_target_pairs={{16,0},{32,16},{48,32},{64,48},{80,64},{96,80},{112,96},{17,1},{33... | collective-permute-start | bytes 49928 | tf_op jit(solution)/shard_map/ppermute | solution.py:24
  105.2 14.6 %collective-permute-start.7 = (f32[4,8,130,1]{2,1,3,0:T(8,128)S(1)}, f32[4,8,130,1]{2,1,3,0:T(8,128)S(1)}, u32[]{:S(2)}, u32[]{:S(2)}) collective-permute-start(f32[4,8,130,1]{2,1,3,0:T(8,128)S(1)} %copy.59), channel_id=1, source_target_pairs={{0,16},{16,32},{32,48},{48,64},{64,80},{80,96},{96,112},{1,17},{17... | collective-permute-start | bytes 49928 | tf_op jit(solution)/shard_map/ppermute | solution.py:23
  122.4 10.3 %copy-start.23 = (f32[4,8,128,256]{3,1,2,0:T(8,128)S(1)}, f32[4,8,128,256]{3,1,2,0:T(8,128)}, u32[]{:S(2)}) copy-start(f32[4,8,128,256]{3,1,2,0:T(8,128)} %fusion.9) | copy-start | bytes 12582916
  122.4 14.4 %copy-start.21 = (f32[4,8,130,1]{3,1,2,0:T(8,128)S(1)}, f32[4,8,130,1]{3,1,2,0:T(8,128)}, u32[]{:S(2)}) copy-start(f32[4,8,130,1]{3,1,2,0:T(8,128)} %copy.60) | copy-start | bytes 49924
  132.7 5.1 %copy-start.12 = (f32[4,7,128,256]{3,1,2,0:T(8,128)S(1)}, f32[4,7,128,256]{3,1,2,0:T(8,128)}, u32[]{:S(2)}) copy-start(f32[4,7,128,256]{3,1,2,0:T(8,128)} %get-tuple-element.31) | copy-start | bytes 11010052
  132.7 5.7 %copy-start.20 = (f32[4,8,130,1]{3,1,2,0:T(8,128)S(1)}, f32[4,8,130,1]{3,1,2,0:T(8,128)}, u32[]{:S(2)}) copy-start(f32[4,8,130,1]{3,1,2,0:T(8,128)} %copy.58) | copy-start | bytes 49924
  132.7 5.7 %copy-start.27 = (f32[4,1,128,256]{3,1,2,0:T(1,128)S(1)}, f32[4,1,128,256]{3,1,2,0:T(1,128)}, u32[]{:S(2)}) copy-start(f32[4,1,128,256]{3,1,2,0:T(1,128)} %get-tuple-element.32) | copy-start | bytes 1572868
  132.8 5.8 %copy-start.28 = (f32[4,1,128,256]{3,1,2,0:T(1,128)S(1)}, f32[4,1,128,256]{3,1,2,0:T(1,128)}, u32[]{:S(2)}) copy-start(f32[4,1,128,256]{3,1,2,0:T(1,128)} %get-tuple-element.33) | copy-start | bytes 1572868
  (14 other events, 31.2 us)
where the time goes:
time: 180 us; the launch traced here: 179 us
  other arithmetic  82.5 us (46%)
  local copies, waits for them, and re-layouts  48.2 us (27%)
  starting transfers between devices  21.8 us (12%)
  blocking collectives  19.7 us (11%)
  waiting for transfers between devices  5.42 us (3%)
    sub x2, other arithmetic, tendencies(): tendency = diffusion * laplace - advect  20.7 us
    mul x2, other arithmetic, tendencies(): grad_z = 0.5 * (upper_side - lower_side)  20 us
    unnamed x1, blocking collectives  19.7 us
    unnamed x82, local copies, waits for them, and re-layouts  17.4 us
    ppermute x4, starting transfers between devices, extended(): after = lax.ppermute(first, axis, down)  12.5 us
    mul x2, other arithmetic, tendencies(): grad_x = 0.5 * (east_side - west_side)  11.7 us
    slice x5, local copies, waits for them, and re-layouts, extended(): last = lax.slice_in_dim(shard, length - width, length, axis=dim)  10.9 us
    ppermute x4, starting transfers between devices, extended(): before = lax.ppermute(last, axis, up)  9.28 us
  transfers between devices with their start and end apart: 8, of which 1 were waited for; matrix products, arithmetic and copies ran while one was open for 18% of the time, Pallas kernels for 0%

commit v1 on v0

v1 whole, which is shorter than its diff:
```python
import math

import jax
import jax.numpy as jnp
from jax import lax
from jax.experimental import pallas as pl
from jax.experimental.pallas import tpu as pltpu
from jax.sharding import PartitionSpec as P

MESH = pl.DeviceIdType.MESH
NX, NY, LANES = 8, 128, 128
NGZ, NGY = 8, 16
UNROLL = 2
F32 = jnp.float32


def lane_index():
    return lax.broadcasted_iota(jnp.int32, (NX, LANES), 1)


def advance(c, e, w, n, s, u, l):
    dx = [e[i] - w[i] for i in range(4)]
    dy = [n[i] - s[i] for i in range(4)]
    dz = [u[i] - l[i] for i in range(4)]
    shear_a = dy[1] + dx[2]
    shear_b = dz[1] + dx[3]
    shear_c = dz[2] + dy[3]
    normal = dx[1] * dx[1] + dy[2] * dy[2] + dz[3] * dz[3]
    shear = shear_a * shear_a + shear_b * shear_b + shear_c * shear_c
    arg = 4.5e-6 * normal + 2.25e-6 * shear + 9e-8
    eddy = arg * lax.rsqrt(arg)
    k_vel = eddy + 0.005
    k_heat = 2.5 * eddy + 0.005
    rest_vel = 1.0 - 6.0 * k_vel
    rest_heat = 1.0 - 6.0 * k_heat
    au = -0.05 * c[1]
    av = -0.05 * c[2]
    aw = -0.05 * c[3]
    out = []
    for i in range(4):
        around = (e[i] + w[i]) + (n[i] + s[i]) + (u[i] + l[i])
        k, rest = (k_heat, rest_heat) if i == 0 else (k_vel, rest_vel)
        out.append(k * around + rest * c[i] + (au * dx[i] + av * dy[i] + aw * dz[i]))
    out[3] = out[3] + 0.05 * c[0]
    return out


def around_x(v):
    return pltpu.roll(v, NX - 1, 0), pltpu.roll(v, 1, 0)


def kernel(
    t_hbm, u_hbm, v_hbm, w_hbm, m_hbm,
    t_out, u_out, v_out, w_out, path_out,
    s0, s1, mk, own, got, corner, got_corner, ring, part, got_part, res,
    in_sem, out_sem, ysend, yrecv, zsend, zrecv, csend, crecv, psend, precv,
):
    gz = lax.axis_index("gz")
    gy = lax.axis_index("gy")
    zup, zdn = lax.rem(gz + 1, NGZ), lax.rem(gz + NGZ - 1, NGZ)
    yup, ydn = lax.rem(gy + 1, NGY), lax.rem(gy + NGY - 1, NGY)
    lane = lane_index()
    first, last = lane == 0, lane == LANES - 1

    barrier = pltpu.get_barrier_semaphore()
    partners = [(gz, yup), (gz, ydn), (zup, yup), (zup, ydn), (zdn, yup), (zdn, ydn)]
    partners += [(lax.rem(gz + d, NGZ), gy) for d in range(1, NGZ)]
    for a, b in partners:
        pl.semaphore_signal(barrier, inc=1, device_id=(a, b), device_id_type=MESH)

    srcs = (t_hbm, u_hbm, v_hbm, w_hbm)
    for f in range(4):
        for h in range(2):
            for x in range(NX):
                pltpu.make_async_copy(
                    srcs[f].at[x, :, pl.ds(h * LANES, LANES)],
                    s0.at[f, h, pl.ds(2, NY), x, :],
                    in_sem.at[f],
                ).start()
    for h in range(2):
        for x in range(NX):
            pltpu.make_async_copy(
                m_hbm.at[x, :, pl.ds(h * LANES, LANES)],
                mk.at[h, pl.ds(1, NY), x, :],
                in_sem.at[4],
            ).start()

    zero = jnp.zeros((NX, LANES), F32)

    def pack(load):
        def body(y, carry):
            l0, l1, r0, r1 = carry
            a, b = load(0, y), load(1, y)
            ra = pltpu.roll(a, y, 1)
            rb = pltpu.roll(b, y + 1, 1)
            here = lane == y
            l0 = jnp.where(here, ra, l0)
            l1 = jnp.where(lane == lax.rem(y + 1, LANES), ra, l1)
            r1 = jnp.where(here, rb, r1)
            r0 = jnp.where(lane == lax.rem(y + LANES - 1, LANES), rb, r0)
            return l0, l1, r0, r1

        l0, l1, r0, r1 = lax.fori_loop(0, NY, body, (zero,) * 4, unroll=8)
        return l0, pltpu.roll(l1, LANES - 1, 1), pltpu.roll(r0, 1, 1), r1

    corner_l, corner_r = zero, zero
    for f in range(4):
        whole = s0.at[f, :, pl.ds(2, NY), :, :]
        pltpu.make_async_copy(whole, whole, in_sem.at[f]).wait()
        l0, l1, r0, r1 = pack(lambda h, y, f=f: s0[f, h, y + 2])
        own[0, f, 0] = l0
        own[0, f, 1] = l1
        own[1, f, 0] = r0
        own[1, f, 1] = r1
        corner_l = jnp.where(lane == f, pltpu.roll(l0, f, 1), corner_l)
        corner_l = jnp.where(lane == 124 + f, pltpu.roll(l0, (f + 125) % LANES, 1), corner_l)
        corner_r = jnp.where(lane == f, pltpu.roll(r1, f, 1), corner_r)
        corner_r = jnp.where(lane == 124 + f, pltpu.roll(r1, (f + 125) % LANES, 1), corner_r)
    whole = mk.at[:, pl.ds(1, NY), :, :]
    pltpu.make_async_copy(whole, whole, in_sem.at[4]).wait()
    l0, _, _, r1 = pack(lambda h, y: mk[h, y + 1].astype(F32))
    own[0, 4, 0] = l0
    own[1, 4, 1] = r1
    own[0, 4, 1] = zero
    own[1, 4, 0] = zero
    corner[0] = corner_l
    corner[1] = corner_r

    pl.semaphore_wait(barrier, len(partners))

    def remote(src, dst, ssem, rsem, dev):
        return pltpu.make_async_remote_copy(
            src_ref=src, dst_ref=dst, send_sem=ssem, recv_sem=rsem,
            device_id=dev, device_id_type=MESH,
        )

    z_copies = [
        remote(own.at[0], got.at[1], zsend.at[0], zrecv.at[0], (zdn, gy)),
        remote(own.at[1], got.at[0], zsend.at[1], zrecv.at[1], (zup, gy)),
    ]
    c_copies = [
        remote(corner.at[0], got_corner.at[1, 1], csend.at[0], crecv.at[0], (zdn, ydn)),
        remote(corner.at[0], got_corner.at[1, 0], csend.at[1], crecv.at[1], (zdn, yup)),
        remote(corner.at[1], got_corner.at[0, 1], csend.at[2], crecv.at[2], (zup, ydn)),
        remote(corner.at[1], got_corner.at[0, 0], csend.at[3], crecv.at[3], (zup, yup)),
    ]
    y_copies = [
        remote(s0.at[:, :, pl.ds(2, 2)], s0.at[:, :, pl.ds(NY + 2, 2)], ysend.at[0], yrecv.at[0], (gz, ydn)),
        remote(s0.at[:, :, pl.ds(NY, 2)], s0.at[:, :, pl.ds(0, 2)], ysend.at[1], yrecv.at[1], (gz, yup)),
        remote(mk.at[:, 1], mk.at[:, NY + 1], ysend.at[2], yrecv.at[2], (gz, ydn)),
        remote(mk.at[:, NY], mk.at[:, 0], ysend.at[3], yrecv.at[3], (gz, yup)),
    ]
    for cp in z_copies + c_copies + y_copies:
        cp.start()
    for cp in z_copies:
        cp.wait()

    bottom, top = gz == 0, gz == NGZ - 1
    for f in range(4):
        for i in range(2):
            got[0, f, i] = jnp.where(bottom, 0.0, got[0, f, i])
            got[1, f, i] = jnp.where(top, 0.0, got[1, f, i])

    def rows(src, j, below, above):
        halves = []
        ca = [src[f, 0, j] for f in range(4)]
        cb = [src[f, 1, j] for f in range(4)]
        ap = [pltpu.roll(v, 1, 1) for v in ca]
        bp = [pltpu.roll(v, 1, 1) for v in cb]
        am = [pltpu.roll(v, LANES - 1, 1) for v in ca]
        bm = [pltpu.roll(v, LANES - 1, 1) for v in cb]
        for h, c in ((0, ca), (1, cb)):
            if h == 0:
                lo = [jnp.where(first, below[f], ap[f]) for f in range(4)]
                up = [jnp.where(last, bm[f], am[f]) for f in range(4)]
            else:
                lo = [jnp.where(first, ap[f], bp[f]) for f in range(4)]
                up = [jnp.where(last, above[f], bm[f]) for f in range(4)]
            ew = [around_x(v) for v in c]
            n = [src[f, h, j + 1] for f in range(4)]
            s = [src[f, h, j - 1] for f in range(4)]
            halves.append(advance(c, [p[0] for p in ew], [p[1] for p in ew], n, s, up, lo))
        return ca, cb, halves

    def row_one(y, ends):
        below, above = ends
        halves = rows(s0, y + 2, below, above)[2]
        for h in range(2):
            m = mk[h, y + 1].astype(F32)
            s1[0, h, y + 1] = halves[h][0]
            for f in range(1, 4):
                s1[f, h, y + 1] = halves[h][f] * m

    def loop_one(y, carry):
        to_first = lax.rem(LANES - y, LANES)
        below = [pltpu.roll(got[0, f, 1], to_first, 1) for f in range(4)]
        above = [pltpu.roll(got[1, f, 0], LANES - 1 - y, 1) for f in range(4)]
        row_one(y, (below, above))
        return carry

    lax.fori_loop(1, NY - 1, loop_one, 0, unroll=UNROLL)

    for cp in c_copies + y_copies:
        cp.wait()
    loop_one(0, 0)
    loop_one(NY - 1, 0)

    ends = []
    for side in range(2):
        for f in range(4):
            lo = pltpu.roll(got_corner[side, 0], (3 - f) % LANES, 1)
            hi = pltpu.roll(got_corner[side, 1], (LANES - f) % LANES, 1)
            v = jnp.where(last, lo, hi)
            ends.append(jnp.where(bottom if side == 0 else top, 0.0, v))
    end_of = lambda side, f: ends[side * 4 + f]

    row_one(-1, (
        [pltpu.roll(end_of(0, f), 1, 1) for f in range(4)],
        [end_of(1, f) for f in range(4)],
    ))
    row_one(NY, (
        [end_of(0, f) for f in range(4)],
        [pltpu.roll(end_of(1, f), LANES - 1, 1) for f in range(4)],
    ))
    for side in range(2):
        if side == 0:
            c = [got[0, f, 1] for f in range(4)]
            lo = [got[0, f, 0] for f in range(4)]
            up = [own[0, f, 0] for f in range(4)]
            m = got[0, 4, 1]
        else:
            c = [got[1, f, 0] for f in range(4)]
            lo = [own[1, f, 1] for f in range(4)]
            up = [got[1, f, 1] for f in range(4)]
            m = got[1, 4, 0]
        n = [jnp.where(last, pltpu.roll(end_of(side, f), LANES - 1, 1), pltpu.roll(c[f], LANES - 1, 1)) for f in range(4)]
        s = [jnp.where(first, pltpu.roll(end_of(side, f), 1, 1), pltpu.roll(c[f], 1, 1)) for f in range(4)]
        ew = [around_x(v) for v in c]
        new = advance(c, [p[0] for p in ew], [p[1] for p in ew], n, s, up, lo)
        outside = bottom if side == 0 else top
        for f in range(4):
            v = new[f] if f == 0 else new[f] * m
            ring[side, f] = jnp.where(outside, 0.0, v)

    outs = (t_out, u_out, v_out, w_out)

    def loop_two(y, acc):
        to_first = lax.rem(LANES - y, LANES)
        below = [pltpu.roll(ring[0, f], to_first, 1) for f in range(4)]
        above = [pltpu.roll(ring[1, f], LANES - 1 - y, 1) for f in range(4)]
        halves = rows(s1, y + 1, below, above)[2]
        total = None
        for h in range(2):
            m = 0.5 * mk[h, y + 1].astype(F32)
            for f in range(4):
                v = s0[f, h, y + 2] + halves[h][f]
                v = 0.5 * v if f == 0 else v * m
                res[f, h, y] = v
                if f == 0:
                    r = 1.0 - jnp.exp(-0.125 * v)
                    total = r if total is None else total + r
        return jnp.where(lane == y, jnp.sum(total, axis=1, keepdims=True), acc)

    acc = lax.fori_loop(0, NY, loop_two, zero, unroll=UNROLL)

    for f in range(4):
        for h in range(2):
            for x in range(NX):
                pltpu.make_async_copy(
                    res.at[f, h, :, x, :],
                    outs[f].at[x, :, pl.ds(h * LANES, LANES)],
                    out_sem.at[f],
                ).start()

    part[...] = acc
    copies = []
    for d in range(1, NGZ):
        peer = lax.rem(gz + d, NGZ)
        copies.append(remote(
            part.at[pl.ds(peer, 1)], got_part.at[d - 1], psend.at[d - 1], precv.at[d - 1], (peer, gy),
        ))
    for cp in copies:
        cp.start()
    total = part[pl.ds(gz, 1)]
    for cp in copies:
        cp.wait()
    for d in range(NGZ - 1):
        total = total + got_part[d]
    path_out[...] = total * (8.0 / math.sqrt(2048.0))

    for f in range(4):
        whole = res.at[f]
        pltpu.make_async_copy(whole, whole, out_sem.at[f]).wait()


def on_device(*args):
    block = jax.ShapeDtypeStruct((NX, NY, 2 * LANES), F32)
    anywhere = pl.BlockSpec(memory_space=pl.ANY)
    return pl.pallas_call(
        kernel,
        out_shape=(block, block, block, block, jax.ShapeDtypeStruct((1, NY), F32)),
        in_specs=[anywhere] * 5,
        out_specs=(anywhere,) * 4 + (pl.BlockSpec(memory_space=pltpu.VMEM),),
        scratch_shapes=[
            pltpu.VMEM((4, 2, NY + 4, NX, LANES), F32),
            pltpu.VMEM((4, 2, NY + 2, NX, LANES), F32),
            pltpu.VMEM((2, NY + 2, NX, LANES), jnp.int32),
            pltpu.VMEM((2, 5, 2, NX, LANES), F32),
            pltpu.VMEM((2, 5, 2, NX, LANES), F32),
            pltpu.VMEM((2, NX, LANES), F32),
            pltpu.VMEM((2, 2, NX, LANES), F32),
            pltpu.VMEM((2, 4, NX, LANES), F32),
            pltpu.VMEM((NX, LANES), F32),
            pltpu.VMEM((NGZ - 1, 1, LANES), F32),
            pltpu.VMEM((4, 2, NY, NX, LANES), F32),
            pltpu.SemaphoreType.DMA((5,)),
            pltpu.SemaphoreType.DMA((4,)),
            pltpu.SemaphoreType.DMA((4,)),
            pltpu.SemaphoreType.DMA((4,)),
            pltpu.SemaphoreType.DMA((2,)),
            pltpu.SemaphoreType.DMA((2,)),
            pltpu.SemaphoreType.DMA((4,)),
            pltpu.SemaphoreType.DMA((4,)),
            pltpu.SemaphoreType.DMA((NGZ - 1,)),
            pltpu.SemaphoreType.DMA((NGZ - 1,)),
        ],
        compiler_params=pltpu.CompilerParams(collective_id=0, has_side_effects=True),
        name="flow",
    )(*args)


def solution(mesh):
    split = P(None, "gy", "gz")
    return jax.shard_map(
        on_device,
        mesh=mesh,
        in_specs=(split,) * 5,
        out_specs=(split,) * 4 + (P("gz", "gy"),),
        check_vma=False,
    )
```

time: 180 us -> 52.5 us (0.29)
  other arithmetic: 82.5 us -> 0 us
  Pallas kernels: 0 us -> 44.6 us
  local copies, waits for them, and re-layouts: 48.2 us -> 7.05 us
  starting transfers between devices: 21.8 us -> 0 us
  blocking collectives: 19.7 us -> 0 us
  waiting for transfers between devices: 5.42 us -> 0 us
    pallas_call x0 -> x1, Pallas kernels: none -> 44.6 us  [on_device(): pl.pallas_call(kernel, out_shape=(block, block, block, block, jax.ShapeDt...]
    mul x11 -> x0, other arithmetic: 44.4 us -> none  [the longest x2 20 us: tendencies(): grad_z = 0.5 * (upper_side - lower_side)]
    ppermute x8 -> x0, starting transfers between devices: 21.8 us -> none  [the longest x4 12.5 us: extended(): after = lax.ppermute(first, axis, down)]
    sub x2 -> x0, other arithmetic: 20.7 us -> none  [tendencies(): tendency = diffusion * laplace - advect]
    unnamed x1 -> x0, blocking collectives: 19.7 us -> none
    slice x12 -> x0, local copies, waits for them, and re-layouts: 18.5 us -> none  [the longest x5 10.9 us: extended(): last = lax.slice_in_dim(shard, length - width, length, axis=dim)]
    unnamed x82 -> x13, local copies, waits for them, and re-layouts: 17.4 us -> 7.05 us
    ppermute x4 -> x0, local copies, waits for them, and re-layouts: 10.3 us -> none  [the longest x2 5.18 us: extended(): before = lax.ppermute(last, axis, up)]
  transfers between devices with their start and end apart: 8 -> 0, of which waited for: 1 -> 0; matrix products, arithmetic and copies ran while one was open for 18% -> 0% of each run, Pallas kernels for 0% -> 0%
where the time goes in v1:
time: 52.5 us; the launch traced here: 52.3 us
  Pallas kernels  44.6 us (85%)
  local copies, waits for them, and re-layouts  7.05 us (13%)
  between operations  0.65 us (1%)
    pallas_call x1, Pallas kernels, on_device(): pl.pallas_call(kernel, out_shape=(block, block, block, block, jax.ShapeDt...  44.6 us
    unnamed x13, local copies, waits for them, and re-layouts  7.05 us

profile of v1, /device:TPU:0, one launch (start us, length us, event | category | flops | bytes accessed | tf_op | source)
XLA Modules:
  0.0 52.3 jit_solution(7037718708874302737)
XLA Ops:
  0.6 44.6 %flow.1 = (f32[8,128,256]{2,1,0:T(8,128)}, f32[8,128,256]{2,1,0:T(8,128)}, f32[8,128,256]{2,1,0:T(8,128)}, f32[8,128,256]{2,1,0:T(8,128)}, f32[1,128]{1,0:T(1,128)}) custom-call(f32[8,128,256]{2,1,0:T(8,128)} %t_hbm.1, f32[8,128,256]{2,1,0:T(8,128)} %u_hbm.1, f32[8,128,256]{2,1,0:T(8,128)} %v_hbm.1, f32[8,128,256]{2,1,0:T(8,128)} %w_hbm.1, s32[8,128,256]{2,1,0:T(8,128)} %m_hbm.1), custom_call_target="tpu_custom_call" | custom-call | tf_op jit(solution)/shard_map/flow/pallas_call | solution.py:299
  45.2 0.0 copy-start.2
  45.2 2.4 %copy.15 = f32[8,128,256]{2,1,0:T(8,128)} copy(f32[8,128,256]{2,1,0:T(8,128)} %get-tuple-element.10) | data formatting | bytes 2097152
  47.6 0.0 copy-done.2
  47.6 0.0 copy-start.1
  47.6 1.0 %copy.16 = f32[8,128,256]{2,1,0:T(8,128)} copy(f32[8,128,256]{2,1,0:T(8,128)S(1)} %copy-done.2) | data formatting | bytes 2097152
  48.6 0.6 %copy-done.1 = f32[8,128,256]{2,1,0:T(8,128)S(1)} copy-done((f32[8,128,256]{2,1,0:T(8,128)S(1)}, f32[8,128,256]{2,1,0:T(8,128)}, u32[]{:S(2)}) %copy-start.1) | copy-done | bytes 1048600
  49.2 0.0 copy-start
  49.2 1.0 %copy.17 = f32[8,128,256]{2,1,0:T(8,128)} copy(f32[8,128,256]{2,1,0:T(8,128)S(1)} %copy-done.1) | data formatting | bytes 2097152
  50.2 0.6 %copy-done = f32[8,128,256]{2,1,0:T(8,128)S(1)} copy-done((f32[8,128,256]{2,1,0:T(8,128)S(1)}, f32[8,128,256]{2,1,0:T(8,128)}, u32[]{:S(2)}) %copy-start) | copy-done | bytes 1048600
  50.8 0.0 copy-start.3
  50.8 1.0 %copy.18 = f32[8,128,256]{2,1,0:T(8,128)} copy(f32[8,128,256]{2,1,0:T(8,128)S(1)} %copy-done) | data formatting | bytes 2097152
  51.8 0.0 copy-done.3
  51.8 0.5 copy.19
Async XLA Ops:
  45.2 2.4 %copy-start.2 = (f32[8,128,256]{2,1,0:T(8,128)S(1)}, f32[8,128,256]{2,1,0:T(8,128)}, u32[]{:S(2)}) copy-start(f32[8,128,256]{2,1,0:T(8,128)} %get-tuple-element.11) | copy-start | bytes 3145732
  47.6 1.6 %copy-start.1 = (f32[8,128,256]{2,1,0:T(8,128)S(1)}, f32[8,128,256]{2,1,0:T(8,128)}, u32[]{:S(2)}) copy-start(f32[8,128,256]{2,1,0:T(8,128)} %get-tuple-element.12) | copy-start | bytes 3145732
  49.2 1.6 %copy-start = (f32[8,128,256]{2,1,0:T(8,128)S(1)}, f32[8,128,256]{2,1,0:T(8,128)}, u32[]{:S(2)}) copy-start(f32[8,128,256]{2,1,0:T(8,128)} %get-tuple-element.13) | copy-start | bytes 3145732
  50.8 1.0 %copy-start.3 = (f32[1,128]{1,0:T(1,128)S(1)}, f32[1,128]{1,0:T(1,128)}, u32[]{:S(2)}) copy-start(f32[1,128]{1,0:T(1,128)} %get-tuple-element.14) | copy-start | bytes 1540

commit v2 on v1

--- a/solution.py
+++ b/solution.py
@@ -51,9 +51,9 @@
 
 def kernel(
     t_hbm, u_hbm, v_hbm, w_hbm, m_hbm,
-    t_out, u_out, v_out, w_out, path_out,
-    s0, s1, mk, own, got, corner, got_corner, ring, part, got_part, res,
-    in_sem, out_sem, ysend, yrecv, zsend, zrecv, csend, crecv, psend, precv,
+    res, path,
+    s0, s1, mk, own, zsrc, got, merged, edges, corner, got_corner, ring, part, got_part,
+    in_sem, ysend, yrecv, zsend, zrecv, csend, crecv, psend, precv,
 ):
     gz = lax.axis_index("gz")
     gy = lax.axis_index("gy")
@@ -86,43 +86,44 @@
             ).start()
 
     zero = jnp.zeros((NX, LANES), F32)
-
-    def pack(load):
-        def body(y, carry):
-            l0, l1, r0, r1 = carry
-            a, b = load(0, y), load(1, y)
-            ra = pltpu.roll(a, y, 1)
-            rb = pltpu.roll(b, y + 1, 1)
-            here = lane == y
-            l0 = jnp.where(here, ra, l0)
-            l1 = jnp.where(lane == lax.rem(y + 1, LANES), ra, l1)
-            r1 = jnp.where(here, rb, r1)
-            r0 = jnp.where(lane == lax.rem(y + LANES - 1, LANES), rb, r0)
-            return l0, l1, r0, r1
-
-        l0, l1, r0, r1 = lax.fori_loop(0, NY, body, (zero,) * 4, unroll=8)
-        return l0, pltpu.roll(l1, LANES - 1, 1), pltpu.roll(r0, 1, 1), r1
+    low2 = (lane & 3) < 2
+    left = lane < LANES // 2
+
+    def pack(f, load):
+        def body(k, carry):
+            groups = []
+            for g in range(4):
+                acc = None
+                for j in range(8 * g, 8 * g + 8):
+                    y = 4 * j + k
+                    both = jnp.where(left, load(0, y), load(1, y))
+                    r = pltpu.roll(both, (4 * j + 2) % LANES, 1)
+                    acc = r if acc is None else jnp.where(lane >= 4 * j, r, acc)
+                groups.append(acc)
+            a = jnp.where(lane >= 32, groups[1], groups[0])
+            b = jnp.where(lane >= 96, groups[3], groups[2])
+            own[f, k] = jnp.where(lane >= 64, b, a).astype(F32)
+            return carry
+
+        lax.fori_loop(0, 4, body, 0)
 
     corner_l, corner_r = zero, zero
     for f in range(4):
         whole = s0.at[f, :, pl.ds(2, NY), :, :]
         pltpu.make_async_copy(whole, whole, in_sem.at[f]).wait()
-        l0, l1, r0, r1 = pack(lambda h, y, f=f: s0[f, h, y + 2])
-        own[0, f, 0] = l0
-        own[0, f, 1] = l1
-        own[1, f, 0] = r0
-        own[1, f, 1] = r1
-        corner_l = jnp.where(lane == f, pltpu.roll(l0, f, 1), corner_l)
-        corner_l = jnp.where(lane == 124 + f, pltpu.roll(l0, (f + 125) % LANES, 1), corner_l)
-        corner_r = jnp.where(lane == f, pltpu.roll(r1, f, 1), corner_r)
-        corner_r = jnp.where(lane == 124 + f, pltpu.roll(r1, (f + 125) % LANES, 1), corner_r)
+        pack(f, lambda h, y, f=f: s0[f, h, y + 2])
+        corner_l = jnp.where(lane == f, pltpu.roll(s0[f, 0, 2], f, 1), corner_l)
+        corner_l = jnp.where(lane == 124 + f, pltpu.roll(s0[f, 0, NY + 1], 124 + f, 1), corner_l)
+        corner_r = jnp.where(lane == f, pltpu.roll(s0[f, 1, 2], f + 1, 1), corner_r)
+        corner_r = jnp.where(lane == 124 + f, pltpu.roll(s0[f, 1, NY + 1], (125 + f) % LANES, 1), corner_r)
     whole = mk.at[:, pl.ds(1, NY), :, :]
     pltpu.make_async_copy(whole, whole, in_sem.at[4]).wait()
-    l0, _, _, r1 = pack(lambda h, y: mk[h, y + 1].astype(F32))
-    own[0, 4, 0] = l0
-    own[1, 4, 1] = r1
-    own[0, 4, 1] = zero
-    own[1, 4, 0] = zero
+    pack(4, lambda h, y: mk[h, y + 1])
+    for f in range(5):
+        for p in range(2):
+            even, odd = own[f, 2 * p], own[f, 2 * p + 1]
+            zsrc[0, f, p] = jnp.where(low2, pltpu.roll(even, LANES - 2, 1), odd)
+            zsrc[1, f, p] = jnp.where(low2, even, pltpu.roll(odd, 2, 1))
     corner[0] = corner_l
     corner[1] = corner_r
 
@@ -135,8 +136,8 @@
         )
 
     z_copies = [
-        remote(own.at[0], got.at[1], zsend.at[0], zrecv.at[0], (zdn, gy)),
-        remote(own.at[1], got.at[0], zsend.at[1], zrecv.at[1], (zup, gy)),
+        remote(zsrc.at[0], got.at[1], zsend.at[0], zrecv.at[0], (zdn, gy)),
+        remote(zsrc.at[1], got.at[0], zsend.at[1], zrecv.at[1], (zup, gy)),
     ]
     c_copies = [
         remote(corner.at[0], got_corner.at[1, 1], csend.at[0], crecv.at[0], (zdn, ydn)),
@@ -152,14 +153,7 @@
     ]
     for cp in z_copies + c_copies + y_copies:
         cp.start()
-    for cp in z_copies:
-        cp.wait()
-
     bottom, top = gz == 0, gz == NGZ - 1
-    for f in range(4):
-        for i in range(2):
-            got[0, f, i] = jnp.where(bottom, 0.0, got[0, f, i])
-            got[1, f, i] = jnp.where(top, 0.0, got[1, f, i])
 
     def rows(src, j, below, above):
         halves = []
@@ -171,11 +165,11 @@
         bm = [pltpu.roll(v, LANES - 1, 1) for v in cb]
         for h, c in ((0, ca), (1, cb)):
             if h == 0:
-                lo = [jnp.where(first, below[f], ap[f]) for f in range(4)]
+                lo = ap if below is None else [jnp.where(first, below[f], ap[f]) for f in range(4)]
                 up = [jnp.where(last, bm[f], am[f]) for f in range(4)]
             else:
                 lo = [jnp.where(first, ap[f], bp[f]) for f in range(4)]
-                up = [jnp.where(last, above[f], bm[f]) for f in range(4)]
+                up = bm if above is None else [jnp.where(last, above[f], bm[f]) for f in range(4)]
             ew = [around_x(v) for v in c]
             n = [src[f, h, j + 1] for f in range(4)]
             s = [src[f, h, j - 1] for f in range(4)]
@@ -192,15 +186,12 @@
                 s1[f, h, y + 1] = halves[h][f] * m
 
     def loop_one(y, carry):
-        to_first = lax.rem(LANES - y, LANES)
-        below = [pltpu.roll(got[0, f, 1], to_first, 1) for f in range(4)]
-        above = [pltpu.roll(got[1, f, 0], LANES - 1 - y, 1) for f in range(4)]
-        row_one(y, (below, above))
+        row_one(y, (None, None))
         return carry
 
     lax.fori_loop(1, NY - 1, loop_one, 0, unroll=UNROLL)
 
-    for cp in c_copies + y_copies:
+    for cp in z_copies + c_copies + y_copies:
         cp.wait()
     loop_one(0, 0)
     loop_one(NY - 1, 0)
@@ -223,32 +214,64 @@
         [pltpu.roll(end_of(1, f), LANES - 1, 1) for f in range(4)],
     ))
     for side in range(2):
-        if side == 0:
-            c = [got[0, f, 1] for f in range(4)]
-            lo = [got[0, f, 0] for f in range(4)]
-            up = [own[0, f, 0] for f in range(4)]
-            m = got[0, 4, 1]
-        else:
-            c = [got[1, f, 0] for f in range(4)]
-            lo = [own[1, f, 1] for f in range(4)]
-            up = [got[1, f, 1] for f in range(4)]
-            m = got[1, 4, 0]
-        n = [jnp.where(last, pltpu.roll(end_of(side, f), LANES - 1, 1), pltpu.roll(c[f], LANES - 1, 1)) for f in range(4)]
-        s = [jnp.where(first, pltpu.roll(end_of(side, f), 1, 1), pltpu.roll(c[f], 1, 1)) for f in range(4)]
-        ew = [around_x(v) for v in c]
-        new = advance(c, [p[0] for p in ew], [p[1] for p in ew], n, s, up, lo)
-        outside = bottom if side == 0 else top
+        for f in range(5):
+            for k in range(4):
+                g = got[side, f, k // 2]
+                if side == 0 and k % 2 == 1:
+                    g = pltpu.roll(g, LANES - 2, 1)
+                if side == 1 and k % 2 == 0:
+                    g = pltpu.roll(g, 2, 1)
+                if f < 4:
+                    g = jnp.where(bottom if side == 0 else top, 0.0, g)
+                near = own[f, k]
+                merged[side, f, k + 1] = jnp.where(low2, g, near) if side == 0 else jnp.where(low2, near, g)
         for f in range(4):
-            v = new[f] if f == 0 else new[f] * m
-            ring[side, f] = jnp.where(outside, 0.0, v)
-
-    outs = (t_out, u_out, v_out, w_out)
+            end = end_of(side, f)
+            before = jnp.where(lane == 1 + side, pltpu.roll(end, 2 + side, 1), pltpu.roll(s0[f, side, 1], 2, 1))
+            after = jnp.where(
+                lane == 125 + side, pltpu.roll(end, 125 + side, 1), pltpu.roll(s0[f, side, NY + 2], 126, 1)
+            )
+            merged[side, f, 0] = jnp.where(lane < 4, before, pltpu.roll(merged[side, f, 4], 4, 1))
+            merged[side, f, 5] = jnp.where(lane >= 124, after, pltpu.roll(merged[side, f, 1], 124, 1))
+
+        def edge(k, carry, side=side):
+            c = [merged[side, f, k + 1] for f in range(4)]
+            n = [merged[side, f, k + 2] for f in range(4)]
+            s = [merged[side, f, k] for f in range(4)]
+            lo = [pltpu.roll(v, 1, 1) for v in c]
+            up = [pltpu.roll(v, LANES - 1, 1) for v in c]
+            ew = [around_x(v) for v in c]
+            new = advance(c, [p[0] for p in ew], [p[1] for p in ew], n, s, up, lo)
+            m = merged[side, 4, k + 1]
+            for f in range(4):
+                edges[side, f, k] = new[f] if f == 0 else new[f] * m
+            return carry
+
+        lax.fori_loop(0, 4, edge, 0, unroll=2)
+
+    def unpack(k, carry):
+        for f in range(4):
+            b, t = edges[0, f, k], edges[1, f, k]
+            inner = jnp.where(low2, t, b)
+            outer = jnp.where(
+                low2,
+                jnp.where(top, 0.0, pltpu.roll(t, LANES - 1, 1)),
+                jnp.where(bottom, 0.0, pltpu.roll(b, 1, 1)),
+            )
+            for j in range(32):
+                y = 4 * j + k
+                shift = (2 * LANES - 4 * j - 2) % LANES
+                v = pltpu.roll(inner, shift, 1)
+                s1[f, 0, y + 1] = jnp.where(first, v, s1[f, 0, y + 1])
+                s1[f, 1, y + 1] = jnp.where(last, v, s1[f, 1, y + 1])
+                ring[f, y] = pltpu.roll(outer, shift, 1)
+        return carry
+
+    lax.fori_loop(0, 4, unpack, 0)
 
     def loop_two(y, acc):
-        to_first = lax.rem(LANES - y, LANES)
-        below = [pltpu.roll(ring[0, f], to_first, 1) for f in range(4)]
-        above = [pltpu.roll(ring[1, f], LANES - 1 - y, 1) for f in range(4)]
-        halves = rows(s1, y + 1, below, above)[2]
+        past = [ring[f, y] for f in range(4)]
+        halves = rows(s1, y + 1, past, past)[2]
         total = None
         for h in range(2):
             m = 0.5 * mk[h, y + 1].astype(F32)
@@ -262,15 +285,6 @@
         return jnp.where(lane == y, jnp.sum(total, axis=1, keepdims=True), acc)
 
     acc = lax.fori_loop(0, NY, loop_two, zero, unroll=UNROLL)
-
-    for f in range(4):
-        for h in range(2):
-            for x in range(NX):
-                pltpu.make_async_copy(
-                    res.at[f, h, :, x, :],
-                    outs[f].at[x, :, pl.ds(h * LANES, LANES)],
-                    out_sem.at[f],
-                ).start()
 
     part[...] = acc
     copies = []
@@ -286,8 +300,20 @@
         cp.wait()
     for d in range(NGZ - 1):
         total = total + got_part[d]
-    path_out[...] = total * (8.0 / math.sqrt(2048.0))
-
+    path[...] = total * (8.0 / math.sqrt(2048.0))
+
+
+def emit(res, path, t_out, u_out, v_out, w_out, path_out, out_sem):
+    outs = (t_out, u_out, v_out, w_out)
+    for f in range(4):
+        for h in range(2):
+            for x in range(NX):
+                pltpu.make_async_copy(
+                    res.at[f, h, :, x, :],
+                    outs[f].at[x, :, pl.ds(h * LANES, LANES)],
+                    out_sem.at[f],
+                ).start()
+    path_out[...] = path[...]
     for f in range(4):
         whole = res.at[f]
         pltpu.make_async_copy(whole, whole, out_sem.at[f]).wait()
@@ -295,26 +321,29 @@
 
 def on_device(*args):
     block = jax.ShapeDtypeStruct((NX, NY, 2 * LANES), F32)
+    line = jax.ShapeDtypeStruct((1, NY), F32)
     anywhere = pl.BlockSpec(memory_space=pl.ANY)
-    return pl.pallas_call(
+    inside = pl.BlockSpec(memory_space=pltpu.VMEM)
+    res, path = pl.pallas_call(
         kernel,
-        out_shape=(block, block, block, block, jax.ShapeDtypeStruct((1, NY), F32)),
+        out_shape=(pltpu.VMEM((4, 2, NY, NX, LANES), F32), pltpu.VMEM((1, NY), F32)),
         in_specs=[anywhere] * 5,
-        out_specs=(anywhere,) * 4 + (pl.BlockSpec(memory_space=pltpu.VMEM),),
+        out_specs=(inside, inside),
         scratch_shapes=[
             pltpu.VMEM((4, 2, NY + 4, NX, LANES), F32),
             pltpu.VMEM((4, 2, NY + 2, NX, LANES), F32),
             pltpu.VMEM((2, NY + 2, NX, LANES), jnp.int32),
+            pltpu.VMEM((5, 4, NX, LANES), F32),
             pltpu.VMEM((2, 5, 2, NX, LANES), F32),
             pltpu.VMEM((2, 5, 2, NX, LANES), F32),
+            pltpu.VMEM((2, 5, 6, NX, LANES), F32),
+            pltpu.VMEM((2, 4, 4, NX, LANES), F32),
             pltpu.VMEM((2, NX, LANES), F32),
             pltpu.VMEM((2, 2, NX, LANES), F32),
-            pltpu.VMEM((2, 4, NX, LANES), F32),
+            pltpu.VMEM((4, NY, NX, LANES), F32),
             pltpu.VMEM((NX, LANES), F32),
             pltpu.VMEM((NGZ - 1, 1, LANES), F32),
-            pltpu.VMEM((4, 2, NY, NX, LANES), F32),
             pltpu.SemaphoreType.DMA((5,)),
-            pltpu.SemaphoreType.DMA((4,)),
             pltpu.SemaphoreType.DMA((4,)),
             pltpu.SemaphoreType.DMA((4,)),
             pltpu.SemaphoreType.DMA((2,)),
@@ -324,9 +353,20 @@
             pltpu.SemaphoreType.DMA((NGZ - 1,)),
             pltpu.SemaphoreType.DMA((NGZ - 1,)),
         ],
-        compiler_params=pltpu.CompilerParams(collective_id=0, has_side_effects=True),
+        compiler_params=pltpu.CompilerParams(
+            collective_id=0, has_side_effects=True, vmem_limit_bytes=59 * 1024 * 1024
+        ),
         name="flow",
     )(*args)
+    return pl.pallas_call(
+        emit,
+        out_shape=(block, block, block, block, line),
+        in_specs=[inside, inside],
+        out_specs=(anywhere,) * 4 + (inside,),
+        scratch_shapes=[pltpu.SemaphoreType.DMA((4,))],
+        compiler_params=pltpu.CompilerParams(vmem_limit_bytes=8 * 1024 * 1024),
+        name="emit",
+    )(res, path)
 
 
 def solution(mesh):

time: 52.5 us -> 38.9 us (0.74)
  local copies, waits for them, and re-layouts: 7.05 us -> 0 us
  Pallas kernels: 44.6 us -> 38.1 us
    unnamed x13 -> x0, local copies, waits for them, and re-layouts: 7.05 us -> none
    pallas_call x1 -> x2, Pallas kernels: 44.6 us -> 38.1 us  [the longest x1 35.6 us: on_device(): pl.pallas_call(kernel, out_shape=(pltpu.VMEM((4, 2, NY, NX, LANES), F32),...]
where the time goes in v2:
time: 38.9 us; the launch traced here: 38.8 us
  Pallas kernels  38.1 us (98%)
  between operations  0.64 us (2%)
    pallas_call x1, Pallas kernels, on_device(): pl.pallas_call(kernel, out_shape=(pltpu.VMEM((4, 2, NY, NX, LANES), F32),...  35.6 us
    pallas_call x1, Pallas kernels, on_device(): pl.pallas_call(emit, out_shape=(block, block, block, block, line), in_spe...  2.51 us

profile of v2, /device:TPU:0, one launch (start us, length us, event | category | flops | bytes accessed | tf_op | source)
XLA Modules:
  0.0 38.8 jit_solution(1469839299625434533)
XLA Ops:
  0.6 35.6 %flow.1 = (f32[4,2,128,8,128]{4,3,2,1,0:T(8,128)S(1)}, f32[1,128]{1,0:T(1,128)S(1)}) custom-call(f32[8,128,256]{2,1,0:T(8,128)} %t_hbm.1, f32[8,128,256]{2,1,0:T(8,128)} %u_hbm.1, f32[8,128,256]{2,1,0:T(8,128)} %v_hbm.1, f32[8,128,256]{2,1,0:T(8,128)} %w_hbm.1, s32[8,128,256]{2,1,0:T(8,128)} %m_hbm.1), custom_call_target="tpu_custom_call" | custom-call | tf_op jit(solution)/shard_map/flow/pallas_call | solution.py:327
  36.3 2.5 %emit.1 = (f32[8,128,256]{2,1,0:T(8,128)}, f32[8,128,256]{2,1,0:T(8,128)}, f32[8,128,256]{2,1,0:T(8,128)}, f32[8,128,256]{2,1,0:T(8,128)}, f32[1,128]{1,0:T(1,128)}) custom-call(f32[4,2,128,8,128]{4,3,2,1,0:T(8,128)S(1)} %get-tuple-element.7.res, f32[1,128]{1,0:T(1,128)S(1)} %get-tuple-element.8.path), custom_call_target="tpu_custom_call" | custom-call | tf_op jit(solution)/shard_map/emit/pallas_call | solution.py:361

commit v3 on v2

--- a/solution.py
+++ b/solution.py
@@ -10,7 +10,8 @@
 MESH = pl.DeviceIdType.MESH
 NX, NY, LANES = 8, 128, 128
 NGZ, NGY = 8, 16
-UNROLL = 2
+UNROLL = 3
+ROWS = 4
 F32 = jnp.float32
 
 
@@ -105,7 +106,7 @@
             own[f, k] = jnp.where(lane >= 64, b, a).astype(F32)
             return carry
 
-        lax.fori_loop(0, 4, body, 0)
+        lax.fori_loop(0, 4, body, 0, unroll=2)
 
     corner_l, corner_r = zero, zero
     for f in range(4):
@@ -269,22 +270,37 @@
 
     lax.fori_loop(0, 4, unpack, 0)
 
-    def loop_two(y, acc):
-        past = [ring[f, y] for f in range(4)]
-        halves = rows(s1, y + 1, past, past)[2]
-        total = None
-        for h in range(2):
-            m = 0.5 * mk[h, y + 1].astype(F32)
-            for f in range(4):
-                v = s0[f, h, y + 2] + halves[h][f]
-                v = 0.5 * v if f == 0 else v * m
-                res[f, h, y] = v
-                if f == 0:
-                    r = 1.0 - jnp.exp(-0.125 * v)
-                    total = r if total is None else total + r
+    def row_sum(y, pair, acc):
+        total = (1.0 - jnp.exp(-0.125 * pair[0])) + (1.0 - jnp.exp(-0.125 * pair[1]))
         return jnp.where(lane == y, jnp.sum(total, axis=1, keepdims=True), acc)
 
-    acc = lax.fori_loop(0, NY, loop_two, zero, unroll=UNROLL)
+    def loop_two(i, carry):
+        acc, warm = carry
+        y0 = i * ROWS
+        new = []
+        for r in range(ROWS):
+            y = y0 + r
+            past = [ring[f, y] for f in range(4)]
+            halves = rows(s1, y + 1, past, past)[2]
+            pair = []
+            for h in range(2):
+                m = 0.5 * mk[h, y + 1].astype(F32)
+                for f in range(4):
+                    v = s0[f, h, y + 2] + halves[h][f]
+                    v = 0.5 * v if f == 0 else v * m
+                    res[f, h, y] = v
+                    if f == 0:
+                        pair.append(v)
+            new.append(tuple(pair))
+        for r in range(ROWS):
+            acc = row_sum(y0 + r - ROWS, warm[r], acc)
+        return acc, tuple(new)
+
+    res[0, 0, 0] = zero
+    blank = res[0, 0, 0]
+    acc, warm = lax.fori_loop(0, NY // ROWS, loop_two, (blank, ((blank, blank),) * ROWS))
+    for r in range(ROWS):
+        acc = row_sum(NY - ROWS + r, warm[r], acc)
 
     part[...] = acc
     copies = []

time: 38.9 us -> 29.8 us (0.77)
  Pallas kernels: 38.1 us -> 29.1 us
    pallas_call x1, Pallas kernels: 35.6 us -> 26.6 us  [on_device(): pl.pallas_call(kernel, out_shape=(pltpu.VMEM((4, 2, NY, NX, LANES), F32),...]
where the time goes in v3:
time: 29.8 us; the launch traced here: 29.7 us
  Pallas kernels  29.1 us (98%)
  between operations  0.64 us (2%)
    pallas_call x1, Pallas kernels, on_device(): pl.pallas_call(kernel, out_shape=(pltpu.VMEM((4, 2, NY, NX, LANES), F32),...  26.6 us
    pallas_call x1, Pallas kernels, on_device(): pl.pallas_call(emit, out_shape=(block, block, block, block, line), in_spe...  2.51 us

profile of v3, /device:TPU:0, one launch (start us, length us, event | category | flops | bytes accessed | tf_op | source)
XLA Modules:
  0.0 29.7 jit_solution(10439336415257570636)
XLA Ops:
  0.6 26.6 %flow.1 = (f32[4,2,128,8,128]{4,3,2,1,0:T(8,128)S(1)}, f32[1,128]{1,0:T(1,128)S(1)}) custom-call(f32[8,128,256]{2,1,0:T(8,128)} %t_hbm.1, f32[8,128,256]{2,1,0:T(8,128)} %u_hbm.1, f32[8,128,256]{2,1,0:T(8,128)} %v_hbm.1, f32[8,128,256]{2,1,0:T(8,128)} %w_hbm.1, s32[8,128,256]{2,1,0:T(8,128)} %m_hbm.1), custom_call_target="tpu_custom_call" | custom-call | tf_op jit(solution)/shard_map/flow/pallas_call | solution.py:343
  27.2 2.5 %emit.1 = (f32[8,128,256]{2,1,0:T(8,128)}, f32[8,128,256]{2,1,0:T(8,128)}, f32[8,128,256]{2,1,0:T(8,128)}, f32[8,128,256]{2,1,0:T(8,128)}, f32[1,128]{1,0:T(1,128)}) custom-call(f32[4,2,128,8,128]{4,3,2,1,0:T(8,128)S(1)} %get-tuple-element.7.res, f32[1,128]{1,0:T(1,128)S(1)} %get-tuple-element.8.path), custom_call_target="tpu_custom_call" | custom-call | tf_op jit(solution)/shard_map/emit/pallas_call | solution.py:377

commit v4 on v3

--- a/solution.py
+++ b/solution.py
@@ -106,7 +106,7 @@
             own[f, k] = jnp.where(lane >= 64, b, a).astype(F32)
             return carry
 
-        lax.fori_loop(0, 4, body, 0, unroll=2)
+        lax.fori_loop(0, 4, body, 0, unroll=4)
 
     corner_l, corner_r = zero, zero
     for f in range(4):

time: 29.8 us -> 29.9 us (level)
  no operation moved by 1% of the time
where the time goes in v4:
time: 29.9 us; the launch traced here: 29.7 us
  Pallas kernels  29.1 us (97%)
  between operations  0.64 us (2%)
    pallas_call x1, Pallas kernels, on_device(): pl.pallas_call(kernel, out_shape=(pltpu.VMEM((4, 2, NY, NX, LANES), F32),...  26.6 us
    pallas_call x1, Pallas kernels, on_device(): pl.pallas_call(emit, out_shape=(block, block, block, block, line), in_spe...  2.51 us

profile of v4, /device:TPU:0, one launch (start us, length us, event | category | flops | bytes accessed | tf_op | source)
XLA Modules:
  0.0 29.7 jit_solution(13275203466111414104)
XLA Ops:
  0.6 26.6 %flow.1 = (f32[4,2,128,8,128]{4,3,2,1,0:T(8,128)S(1)}, f32[1,128]{1,0:T(1,128)S(1)}) custom-call(f32[8,128,256]{2,1,0:T(8,128)} %t_hbm.1, f32[8,128,256]{2,1,0:T(8,128)} %u_hbm.1, f32[8,128,256]{2,1,0:T(8,128)} %v_hbm.1, f32[8,128,256]{2,1,0:T(8,128)} %w_hbm.1, s32[8,128,256]{2,1,0:T(8,128)} %m_hbm.1), custom_call_target="tpu_custom_call" | custom-call | tf_op jit(solution)/shard_map/flow/pallas_call | solution.py:343
  27.2 2.5 %emit.1 = (f32[8,128,256]{2,1,0:T(8,128)}, f32[8,128,256]{2,1,0:T(8,128)}, f32[8,128,256]{2,1,0:T(8,128)}, f32[8,128,256]{2,1,0:T(8,128)}, f32[1,128]{1,0:T(1,128)}) custom-call(f32[4,2,128,8,128]{4,3,2,1,0:T(8,128)S(1)} %get-tuple-element.7.res, f32[1,128]{1,0:T(1,128)S(1)} %get-tuple-element.8.path), custom_call_target="tpu_custom_call" | custom-call | tf_op jit(solution)/shard_map/emit/pallas_call | solution.py:377
